TPU v7x, 256 devices: a whole 4x4x8 slice. The times are simulated.
256 devices in a mesh: expert: 4 (over z_lo), dp: 64 (over y, x, z_hi, core).
Axes of the slice: x: 4, y: 4, z: 8 (z_hi: 2, z_lo: 4; z = z_hi * 4 + z_lo), core: 2. Of those that a mesh axis runs over, the one named last changes fastest.
Arguments:
- act_attn: bfloat16 [65536, 256], P(('expert', 'dp')), may hold values from -10 to 10
- dy_attn: bfloat16 [65536, 6144], P(('expert', 'dp')), may hold values from -10 to 10
- act_exp: bfloat16 [4, 8192, 128], P('expert', 'dp'), may hold values from -10 to 10
- dy_exp: bfloat16 [4, 8192, 6144], P('expert', 'dp'), may hold values from -10 to 10
- w_attn: float32 [256, 6144], P(('expert', 'dp')), may hold values from -0.3 to 0.3
- m_attn: float32 [256, 6144], P(('expert', 'dp')), may hold values from -1.5 to 1.5
- v_attn: float32 [256, 6144], P(('expert', 'dp')), may hold values from 0.05 to 1
- w_exp: float32 [4, 128, 6144], P('expert', 'dp'), may hold values from -0.3 to 0.3
- m_exp: float32 [4, 128, 6144], P('expert', 'dp'), may hold values from -1.5 to 1.5
- v_exp: float32 [4, 128, 6144], P('expert', 'dp'), may hold values from 0.05 to 1
Outputs:
- w_attn_new: float32 [256, 6144], P(('expert', 'dp'))
- m_attn_new: float32 [256, 6144], P(('expert', 'dp'))
- v_attn_new: float32 [256, 6144], P(('expert', 'dp'))
- w_exp_new: float32 [4, 128, 6144], P('expert', 'dp')
- m_exp_new: float32 [4, 128, 6144], P('expert', 'dp')
- v_exp_new: float32 [4, 128, 6144], P('expert', 'dp')
- attn_weights: bfloat16 [256, 6144], replicated
- expert_weights: bfloat16 [4, 128, 6144], P('expert')
All inputs are finite; a program needn't handle non-finite values.
Results may differ from a plain program's by a relative error of at most 0.0075.
Values may be sent and summed in bfloat16 or wider, within the bound.
A program may use at most 64 MiB of HBM per device.

v0:
```python
import math
import jax
import jax.numpy as jnp
from jax import lax
from jax.sharding import PartitionSpec as P

beta_first = 0.9
beta_second = 0.95
bias_first = 1.0 - 0.9**10
bias_second = 1.0 - 0.95**10
learn_rate = 0.01
decay_rate = 0.1
adam_eps = 1e-08


def contract_rows(left, right):
    return lax.dot_general(
        left, right, (((0,), (0,)), ((), ())), preferred_element_type=jnp.float32
    )


def adamw(grad, weight, moment, second, factor):
    scaled = factor * grad
    moment_new = beta_first * moment + (1.0 - beta_first) * scaled
    second_new = beta_second * second + (1.0 - beta_second) * scaled * scaled
    update = moment_new / bias_first / (jnp.sqrt(second_new / bias_second) + adam_eps)
    weight_new = weight - learn_rate * (update + decay_rate * weight)
    return (weight_new, moment_new, second_new)


def body(act_attn, dy_attn, act_exp, dy_exp, w_attn, m_attn, v_attn, w_exp, m_exp, v_exp):
    width = w_attn.shape[1]
    n_expert = lax.axis_size("expert")
    total_params = width * (act_attn.shape[1] + n_expert * act_exp.shape[2])
    limit = 0.5 * math.sqrt(total_params)
    g_attn = lax.psum_scatter(
        contract_rows(act_attn, dy_attn), ("expert", "dp"), scatter_dimension=0, tiled=True
    )
    sq_attn = jnp.sum(g_attn * g_attn)
    local_act = act_exp[0]
    local_dy = dy_exp[0]
    g_exp = lax.psum_scatter(
        contract_rows(local_act, local_dy), "dp", scatter_dimension=0, tiled=True
    )
    sq_exp = jnp.sum(g_exp * g_exp)
    summed = lax.psum((sq_attn, sq_exp), ("expert", "dp"))
    total = summed[0] + summed[1]
    norm = jnp.sqrt(total)
    factor = jnp.minimum(1.0, limit / (norm + 1e-06))
    wa_new, ma_new, va_new = adamw(g_attn, w_attn, m_attn, v_attn, factor)
    we_new, me_new, ve_new = adamw(g_exp[None], w_exp, m_exp, v_exp, factor)
    attn_half = wa_new.astype(jnp.bfloat16)
    attn_full = lax.all_gather(attn_half, ("expert", "dp"), axis=0, tiled=True)
    expert_full = lax.all_gather(we_new.astype(jnp.bfloat16), "dp", axis=1, tiled=True)
    return (wa_new, ma_new, va_new, we_new, me_new, ve_new, attn_full, expert_full)


def solution(mesh):
    return jax.shard_map(
        body,
        mesh=mesh,
        in_specs=(
            P(("expert", "dp"), None),
            P(("expert", "dp"), None),
            P("expert", "dp", None),
            P("expert", "dp", None),
            P(("expert", "dp"), None),
            P(("expert", "dp"), None),
            P(("expert", "dp"), None),
            P("expert", "dp", None),
            P("expert", "dp", None),
            P("expert", "dp", None),
        ),
        out_specs=(
            P(("expert", "dp"), None),
            P(("expert", "dp"), None),
            P(("expert", "dp"), None),
            P("expert", "dp", None),
            P("expert", "dp", None),
            P("expert", "dp", None),
            P(),
            P("expert", None, None),
        ),
        check_vma=False,
    )
```

profile of v0, /device:TPU:32, one launch (start us, length us, event | category | flops | bytes accessed | tf_op | source)
XLA Modules:
  0.0 1681.9 jit_solution(16280890841784815197)
XLA Ops:
  7.2 0.0 copy-start
  7.2 0.0 all-reduce.5.cloned.1.call-start
  7.2 1.8 copy-done
  9.1 4.5 fusion.9
  13.6 0.0 copy-start.4
  13.6 0.0 all-reduce.5.cloned.1.call-update
  13.6 0.0 copy-start.8
  13.6 0.0 copy-start.1
  13.7 0.0 copy-start.2
  13.7 0.0 copy-start.3
  13.7 0.0 copy-start.5
  13.7 0.0 copy-start.6
  13.7 0.0 copy-start.7
  13.7 0.0 all-reduce.7.cloned.1.call-start
  13.8 0.6 copy-done.4
  14.4 3.7 fusion
  18.0 0.0 all-reduce.7.cloned.1.call-update
  18.1 0.0 all-gather.4.cloned.1.call-start
  18.1 0.0 copy-done.8
  18.1 0.6 dynamic-slice.1
  19.4 268.9 %all-reduce.5.cloned.1.call-done = f32[256,6144]{1,0:T(8,128)} async-done(((f32[256,6144]{1,0:T(8,128)}), f32[256,6144]{1,0:T(8,128)}) %all-reduce.5.cloned.1.call-update) | async-done | bytes 6291472
  288.3 1.6 multiply_reduce_fusion.1
  289.9 795.2 %all-reduce.7.cloned.1.call-done = f32[128,6144]{1,0:T(8,128)} async-done(((f32[128,6144]{1,0:T(8,128)}), f32[128,6144]{1,0:T(8,128)}) %all-reduce.7.cloned.1.call-update) | async-done | bytes 3145744
  1085.1 1.6 multiply_reduce_fusion
  1088.0 78.6 %psum.16 = f32[]{:T(128)} all-reduce(f32[]{:T(128)S(6)} %add.44), channel_id=1, replica_groups=mesh['expert'=4,'dp'=64] {'expert','dp'}, use_global_device_ids=true, to_apply=%region_2.0 | all-reduce | flops 1 | bytes 8 | tf_op jit(solution)/shard_map/psum | solution.py:46
  1167.4 0.0 copy-done.1
  1167.4 0.0 copy-done.2
  1167.4 0.0 copy-done.3
  1167.4 1.8 fusion.6
  1169.2 0.7 copy.20
  1169.8 0.0 all-gather.4.cloned.1.call-update
  1169.9 0.0 all-gather.6.cloned.1.call-start
  1169.9 0.0 copy-done.5
  1169.9 0.0 copy-done.6
  1169.9 0.0 copy-done.7
  1169.9 1.8 convert_bitcast_fusion
  1171.7 0.0 all-gather.6.cloned.1.call-update
  1171.7 81.3 %all-gather.4.cloned.1.call-done = bf16[1,128,6144]{2,0,1:T(2,128)(2,1)} async-done(((bf16[1,2,6144]{2,0,1:T(2,128)(2,1)}), bf16[1,128,6144]{2,0,1:T(2,128)(2,1)}) %all-gather.4.cloned.1.call-update) | async-done | bytes 1572880 | tf_op jit(solution)/shard_map/all_gather | solution.py:54
  1253.0 3.9 copy.21
  1256.9 412.2 %all-gather.6.cloned.1.call-done = bf16[256,1,6144]{2,1,0:T(2,128)(2,1)} async-done(((bf16[1,1,6144]{2,1,0:T(2,128)(2,1)}), bf16[256,1,6144]{2,1,0:T(2,128)(2,1)}) %all-gather.6.cloned.1.call-update) | async-done | bytes 3145744 | tf_op jit(solution)/shard_map/all_gather | solution.py:53
  1669.1 6.2 copy.24
Async XLA Ops:
  7.2 1.9 copy-start
  7.2 281.1 %all-reduce.5.cloned.1.call-start = ((), (), s32[]{:S(2)}) async-start(), calls=%async_computation.2 | async-start | bytes 12582912
  13.6 0.8 copy-start.4
  13.6 4.5 copy-start.8
  13.6 1153.7 %copy-start.1 = (f32[1,2,6144]{2,1,0:T(2,128)S(1)}, f32[1,2,6144]{2,1,0:T(2,128)}, u32[]{:S(2)}) copy-start(f32[1,2,6144]{2,1,0:T(2,128)} %param.17) | copy-start | bytes 147460
  13.7 1153.7 %copy-start.2 = (f32[1,2,6144]{2,1,0:T(2,128)S(1)}, f32[1,2,6144]{2,1,0:T(2,128)}, u32[]{:S(2)}) copy-start(f32[1,2,6144]{2,1,0:T(2,128)} %param.18) | copy-start | bytes 147460
  13.7 1153.7 %copy-start.3 = (f32[1,2,6144]{2,1,0:T(2,128)S(1)}, f32[1,2,6144]{2,1,0:T(2,128)}, u32[]{:S(2)}) copy-start(f32[1,2,6144]{2,1,0:T(2,128)} %param.19) | copy-start | bytes 147460
  13.7 1156.2 %copy-start.5 = (f32[1,6144]{1,0:T(1,128)S(1)}, f32[1,6144]{1,0:T(1,128)}, u32[]{:S(2)}) copy-start(f32[1,6144]{1,0:T(1,128)} %param.14) | copy-start | bytes 73732
  13.7 1156.2 %copy-start.6 = (f32[1,6144]{1,0:T(1,128)S(1)}, f32[1,6144]{1,0:T(1,128)}, u32[]{:S(2)}) copy-start(f32[1,6144]{1,0:T(1,128)} %param.15) | copy-start | bytes 73732
  13.7 1156.2 %copy-start.7 = (f32[1,6144]{1,0:T(1,128)S(1)}, f32[1,6144]{1,0:T(1,128)}, u32[]{:S(2)}) copy-start(f32[1,6144]{1,0:T(1,128)} %param.16) | copy-start | bytes 73732
  13.7 1071.4 %all-reduce.7.cloned.1.call-start = ((), (), s32[]{:S(2)}) async-start(), calls=%async_computation.3 | async-start | bytes 6291456
  18.1 1234.9 %all-gather.4.cloned.1.call-start = ((), (), s32[]{:S(2)}) async-start(), calls=%async_computation | async-start | bytes 3194880 | tf_op jit(solution)/shard_map/all_gather | solution.py:54
  1169.9 499.3 %all-gather.6.cloned.1.call-start = ((), (), s32[]{:S(2)}) async-start(), calls=%async_computation.1 | async-start | bytes 6316032 | tf_op jit(solution)/shard_map/all_gather | solution.py:53
Sparse Core Ops, SparseCore 0:
  13.7 274.5 all-reduce.4
  291.7 793.3 all-reduce.6
  1170.0 82.9 all-gather.3
  1255.3 413.8 all-gather.5
where the time goes:
time: 1680 us
  waiting for transfers between devices  1560 us (93%)
  blocking collectives  78.6 us (5%)
    unnamed x6, waiting for transfers between devices  1060 us
    all_gather x1, waiting for transfers between devices, body(): attn_full = lax.all_gather(attn_half, ('expert', 'dp'), axis=0, tiled=True)  412 us
    all_gather x1, waiting for transfers between devices, body(): lax.all_gather(we_new.astype(jnp.bfloat16), 'dp', axis=1, tiled=True)  81.3 us
    psum x1, blocking collectives, body(): summed = lax.psum((sq_attn, sq_exp), ('expert', 'dp'))  78.6 us
  transfers between devices with their start and end apart: 4, of which 4 were waited for; matrix products, arithmetic and copies ran while one was open for 1% of the time, Pallas kernels for 0%

commit v1 on v0

--- a/solution.py
+++ b/solution.py
@@ -50,7 +50,8 @@
     wa_new, ma_new, va_new = adamw(g_attn, w_attn, m_attn, v_attn, factor)
     we_new, me_new, ve_new = adamw(g_exp[None], w_exp, m_exp, v_exp, factor)
     attn_half = wa_new.astype(jnp.bfloat16)
-    attn_full = lax.all_gather(attn_half, ("expert", "dp"), axis=0, tiled=True)
+    sent = jnp.stack([attn_half] * lax.axis_size(("expert", "dp")))
+    attn_full = jnp.concatenate(lax.all_to_all(sent, ("expert", "dp"), 0, 0), axis=0)
     expert_full = lax.all_gather(we_new.astype(jnp.bfloat16), "dp", axis=1, tiled=True)
     return (wa_new, ma_new, va_new, we_new, me_new, ve_new, attn_full, expert_full)
 

time: 1680 us -> 1350 us (0.80)
  waiting for transfers between devices: 1560 us -> 1160 us
  local copies, waits for them, and re-layouts: 13.9 us -> 46.1 us
  other arithmetic: 6.68 us -> 27.3 us
    all_gather x1 -> x0, waiting for transfers between devices: 412 us -> none  [body(): attn_full = lax.all_gather(attn_half, ('expert', 'dp'), axis=0, tiled=True)]
    unnamed x21 -> x23, local copies, waits for them, and re-layouts: 13.2 us -> 40.6 us
    another operation x0 -> x1, other arithmetic: none -> 20.6 us  [body(): sent = jnp.stack([attn_half] * lax.axis_size(('expert', 'dp')))]
    unnamed x6 -> x5, waiting for transfers between devices: 1060 us -> 1060 us
  transfers between devices with their start and end apart: 4 -> 4, of which waited for: 4 -> 3; matrix products, arithmetic and copies ran while one was open for 1% -> 1% of each run, Pallas kernels for 0% -> 0%
where the time goes in v1:
time: 1350 us
  waiting for transfers between devices  1160 us (86%)
  blocking collectives  78.6 us (6%)
  local copies, waits for them, and re-layouts  46.1 us (3%)
  other arithmetic  27.3 us (2%)
  between operations  16.6 us (1%)
    unnamed x5, waiting for transfers between devices  1060 us
    all_gather x1, waiting for transfers between devices, body(): lax.all_gather(we_new.astype(jnp.bfloat16), 'dp', axis=1, tiled=True)  94.8 us
    psum x1, blocking collectives, body(): summed = lax.psum((sq_attn, sq_exp), ('expert', 'dp'))  78.6 us
    unnamed x23, local copies, waits for them, and re-layouts  40.6 us
  transfers between devices with their start and end apart: 4, of which 3 were waited for; matrix products, arithmetic and copies ran while one was open for 1% of the time, Pallas kernels for 0%

profile of v1, /device:TPU:32, one launch (start us, length us, event | category | flops | bytes accessed | tf_op | source)
XLA Modules:
  0.0 1345.2 jit_solution(14662673738310716801)
XLA Ops:
  7.2 0.0 copy-start
  7.2 0.0 all-reduce.5.cloned.1.call-start
  7.2 1.8 copy-done
  9.1 4.6 fusion.9
  13.6 0.0 copy-start.4
  13.6 0.0 all-reduce.5.cloned.1.call-update
  13.7 0.0 copy-start.8
  13.7 0.0 copy-start.5
  13.7 0.0 copy-start.6
  13.7 0.0 copy-start.7
  13.7 0.0 all-reduce.7.cloned.1.call-start
  13.8 0.6 copy-done.4
  14.4 3.7 fusion
  18.1 0.0 all-reduce.7.cloned.1.call-update
  18.1 0.0 copy-done.8
  18.1 0.6 dynamic-slice.1
  19.3 269.0 %all-reduce.5.cloned.1.call-done = f32[256,6144]{1,0:T(8,128)} async-done(((f32[256,6144]{1,0:T(8,128)}), f32[256,6144]{1,0:T(8,128)}) %all-reduce.5.cloned.1.call-update) | async-done | bytes 6291472
  288.4 1.6 multiply_reduce_fusion.1
  289.9 795.2 %all-reduce.7.cloned.1.call-done = f32[128,6144]{1,0:T(8,128)} async-done(((f32[128,6144]{1,0:T(8,128)}), f32[128,6144]{1,0:T(8,128)}) %all-reduce.7.cloned.1.call-update) | async-done | bytes 3145744
  1085.2 1.6 multiply_reduce_fusion
  1088.1 78.6 %psum.16 = f32[]{:T(128)} all-reduce(f32[]{:T(128)S(6)} %add.44), channel_id=1, replica_groups=mesh['expert'=4,'dp'=64] {'expert','dp'}, use_global_device_ids=true, to_apply=%region_2.0 | all-reduce | flops 1 | bytes 8 | tf_op jit(solution)/shard_map/psum | solution.py:46
  1167.4 0.0 copy-done.5
  1167.4 0.0 copy-done.6
  1167.4 0.0 copy-done.7
  1167.5 1.8 convert_reduce_fusion
  1169.2 4.3 stack.2
  1173.5 0.5 broadcast.30
  1174.0 20.6 %reduce.2 = bf16[256,6144]{1,0:T(8,128)(2,1)} reduce(bf16[256,1,6144]{2,1,0:T(2,128)(2,1)} %stack.2, bf16[]{:T(256)} %broadcast.30), dimensions={1}, to_apply=%stack.2.reduce_sub_computation | reduce | bytes 6291458 | tf_op jit(solution)/shard_map/stack | solution.py:53
  1194.6 8.0 reshape.29
  1202.6 0.0 copy-start.1
  1202.6 0.0 copy-start.2
  1202.7 0.0 copy-start.3
  1202.7 8.9 all-to-all-start
  1211.6 0.2 all-gather.2.cloned.1.call-start
  1211.8 0.0 copy-done.1
  1211.8 0.0 copy-done.2
  1211.8 0.0 copy-done.3
  1211.9 1.8 fusion.6
  1213.6 0.7 copy.20
  1214.3 0.0 all-gather.2.cloned.1.call-update
  1214.3 94.8 %all-gather.2.cloned.1.call-done = bf16[1,128,6144]{2,0,1:T(2,128)(2,1)} async-done(((bf16[1,2,6144]{2,0,1:T(2,128)(2,1)}), bf16[1,128,6144]{2,0,1:T(2,128)(2,1)}) %all-gather.2.cloned.1.call-update) | async-done | bytes 1572880 | tf_op jit(solution)/shard_map/all_gather | solution.py:55
  1309.1 3.9 copy.21
  1313.1 0.0 all-to-all-done
  1313.1 19.3 %reshape.30 = bf16[256,1,6144]{2,1,0:T(2,128)(2,1)} reshape(bf16[256,2,3072]{2,1,0:T(2,128)(2,1)} %all-to-all-done) | data formatting | bytes 6291456
  1332.4 6.2 copy.24
Async XLA Ops:
  7.2 1.9 copy-start
  7.2 281.2 %all-reduce.5.cloned.1.call-start = ((), (), s32[]{:S(2)}) async-start(), calls=%async_computation.2 | async-start | bytes 12582912
  13.6 0.8 copy-start.4
  13.7 4.4 copy-start.8
  13.7 1153.8 %copy-start.5 = (f32[1,6144]{1,0:T(1,128)S(1)}, f32[1,6144]{1,0:T(1,128)}, u32[]{:S(2)}) copy-start(f32[1,6144]{1,0:T(1,128)} %param.14) | copy-start | bytes 73732
  13.7 1153.7 %copy-start.6 = (f32[1,6144]{1,0:T(1,128)S(1)}, f32[1,6144]{1,0:T(1,128)}, u32[]{:S(2)}) copy-start(f32[1,6144]{1,0:T(1,128)} %param.15) | copy-start | bytes 73732
  13.7 1153.7 %copy-start.7 = (f32[1,6144]{1,0:T(1,128)S(1)}, f32[1,6144]{1,0:T(1,128)}, u32[]{:S(2)}) copy-start(f32[1,6144]{1,0:T(1,128)} %param.16) | copy-start | bytes 73732
  13.7 1071.5 %all-reduce.7.cloned.1.call-start = ((), (), s32[]{:S(2)}) async-start(), calls=%async_computation.3 | async-start | bytes 6291456
  1202.6 9.2 copy-start.1
  1202.6 9.2 copy-start.2
  1202.7 9.2 copy-start.3
  1202.7 110.4 %all-to-all-start = ((bf16[256,2,3072]{2,1,0:T(2,128)(2,1)}), bf16[256,2,3072]{2,1,0:T(2,128)(2,1)}, u32[]{:S(2)}, u32[]{:S(2)}) async-start(bf16[256,2,3072]{2,1,0:T(2,128)(2,1)} %reshape.29), calls=%async_computation | async-start | bytes 6291456 | tf_op jit(solution)/shard_map/all_to_all | solution.py:54
  1211.6 97.5 %all-gather.2.cloned.1.call-start = ((), (), s32[]{:S(2)}) async-start(), calls=%async_computation.1 | async-start | bytes 3194880 | tf_op jit(solution)/shard_map/all_gather | solution.py:55
Sparse Core Ops, SparseCore 0:
  13.8 274.5 all-reduce.4
  291.7 793.3 all-reduce.6
  1216.5 92.5 all-gather.1
